TPU v7x, 32 devices: a whole 2x2x4 slice. The times are simulated.
32 devices in a mesh: section: 4 (over y, core), tensor: 8 (over z, x).
Axes of the slice: x: 2, y: 2, z: 4, core: 2. Of those that a mesh axis runs over, the one named last changes fastest.
Arguments:
- carry_in: bfloat16 [4, 2, 16, 4096], P('section', None, 'tensor'), may hold values from -6 to 6
- norm_gain: float32 [4, 4096], P('section'), may hold values from 0.5 to 1.5
- w_gate: bfloat16 [4, 384, 128, 128], P('section', 'tensor'), may hold values from -0.15625 to 0.15625
- w_up: bfloat16 [4, 384, 128, 128], P('section', 'tensor'), may hold values from -0.15625 to 0.15625
- w_down: bfloat16 [4, 384, 128, 128], P('section', 'tensor'), may hold values from -0.15625 to 0.15625
- tile_list: int32 [4, 384], P('section', 'tensor'), may hold values from 0 to 128, as said below
- grad_in: bfloat16 [4, 2, 16, 4096], P('section', None, 'tensor'), may hold values from -6 to 6
Outputs:
- section_out: bfloat16 [4, 2, 16, 4096], P('section', None, 'tensor')
- grad_back: bfloat16 [4, 2, 16, 4096], P('section', None, 'tensor')
Inputs may be any that keep to these rules, and one draw needn't show every extreme that they name: `tile_list`: for each layer and tensor index t, entries 48 * t to 48 * t + 47 list distinct tile numbers f * 32 + c (f a block of that device's hidden units, c a block of features) in rising order, followed by the padding value 4 * 32. Each such list has at least 24 live entries, and in every layer some tensor index has all 48 live.
All inputs are finite; a program needn't handle non-finite values.
Results may differ from a plain program's by a relative error of at most 0.013.
Values may be sent and summed in bfloat16 or wider, within the bound.
A program may use at most 64 MiB of HBM per device.

v0:
```python
import functools

import jax
import jax.numpy as jnp
from jax import lax
from jax.experimental import pallas as pl
from jax.experimental.pallas import tpu as pltpu
from jax.sharding import PartitionSpec as P

FB_DEV = 4
EPS = 1e-05
PAIR = 2
MESH = pl.DeviceIdType.MESH
NT = (((1,), (1,)), ((), ()))


def kernel(
    sections, tensors,
    tl, carry, gain, wg_h, wu_h, wd_h, dy_h,
    out, gback,
    xg, dyg, dyn, gn, gv, cown, wg, wu, wd, nb, db, xs, gu, dh, part, hb, dgu,
    stage, xr, zs, zr, inv, last, lsem, ssem, rsem,
):
    line = tensors // PAIR
    mb, tokd, width = carry.shape[1:]
    per = mb * tokd
    half = line * per
    rows = PAIR * half
    blk = wg.shape[-1]
    slots = wg.shape[0]
    dblocks = width // blk
    s = lax.axis_index("section")
    t = lax.axis_index("tensor")
    z, x = t // PAIR, t % PAIR
    s_next, s_prev = (s + 1) % sections, (s + sections - 1) % sections

    def dev(sec, d, other=False):
        xx = (PAIR - 1 - x) if other else x
        return (sec, ((z + d) % line) * PAIR + xx)

    local = [
        pltpu.make_async_copy(dy_h.at[0], dyg.at[0, 0], lsem.at[0]),
        pltpu.make_async_copy(wd_h.at[0], wd, lsem.at[1]),
        pltpu.make_async_copy(wg_h.at[0], wg, lsem.at[2]),
        pltpu.make_async_copy(wu_h.at[0], wu, lsem.at[3]),
        pltpu.make_async_copy(gain, gv, lsem.at[4]),
        pltpu.make_async_copy(carry.at[0], cown, lsem.at[5]),
    ]
    for c in local:
        c.start()

    barrier = pltpu.get_barrier_semaphore()
    friends = [dev(s, d) for d in range(1, line)]
    friends += [dev(s_next, d) for d in range(line)]
    friends += [dev(s_prev, d) for d in range(line)]
    friends += [dev(s, 0, True), dev(s_next, 0, True), dev(s_prev, 0, True)]
    for f in friends:
        pl.semaphore_signal(barrier, inc=1, device_id=f, device_id_type=MESH)
    pl.semaphore_wait(barrier, len(friends))

    def remote(src, dst, ssi, rsi, to):
        return pltpu.make_async_remote_copy(
            src_ref=src, dst_ref=dst, send_sem=ssem.at[ssi], recv_sem=rsem.at[rsi],
            device_id=to, device_id_type=MESH,
        )

    DYZ, XZ, DYX, XX = 0, line, 2 * line, 3 * line
    FZ, BZ = 4 * line, 5 * line
    FX, BX, DYB, GNB = 6 * line, 6 * line + 1, 6 * line + 2, 6 * line + 3
    back = lambda d: (line - d) % line
    sent = []

    def go(c):
        c.start()
        sent.append(c)

    mate = dev(s, 0, True)
    order = sorted(range(line), key=lambda d: min(d, line - d))
    for d in order:
        go(remote(carry.at[0], xg.at[0, back(d)], XZ + d, XZ + back(d), dev(s_next, d)))
        if d == 0:
            go(remote(carry.at[0], xg.at[1, 0], XX, XX, dev(s_next, 0, True)))
    go(remote(dy_h.at[0], dyg.at[1, 0], DYX, DYX, mate))
    go(remote(dy_h.at[0], dyn, DYB, DYB, dev(s_prev, 0)))
    go(remote(gain, gn, GNB, GNB, dev(s_prev, 0)))

    p = jnp.int32(0)
    for f in range(FB_DEV):
        def cell(i, p, f=f):
            q = f * dblocks + i
            hit = tl[0, jnp.minimum(p, slots - 1)] == q
            inv[q] = jnp.where(hit, p, slots)
            return p + hit.astype(jnp.int32)
        p_new = lax.fori_loop(0, dblocks, cell, p, unroll=4)
        last[f] = jnp.where(p_new > p, p_new - 1, slots)
        p = p_new
    gu[slots] = jnp.zeros((rows, 2 * blk), jnp.float32)
    dh[slots] = jnp.zeros((rows, blk), jnp.float32)
    part[slots] = jnp.zeros((rows, blk), jnp.float32)

    near = sorted(range(line), key=lambda d: min(d, line - d))
    for d in near:
        remote(carry.at[0], xg.at[0, d], XZ + d, XZ + d, mate).wait_recv()
        if d:
            go(remote(xg.at[0, d], xg.at[1, d], XX + d, XX + d, mate))
    for d in order:
        if d:
            go(remote(dy_h.at[0], dyg.at[0, back(d)], DYZ + d, DYZ + back(d), dev(s, d)))
    for c in local:
        c.wait()

    def rows_of(ref, c, h):
        cols = pl.ds(pl.multiple_of(c * blk, blk), blk)
        pieces = []
        for d in range(line):
            for m in range(mb):
                pieces.append(ref[h, d, m, :, cols].astype(jnp.float32))
        return jnp.concatenate(pieces, axis=0)

    def f_of(k):
        return jnp.minimum(tl[0, k] // dblocks, FB_DEV - 1)

    def c_of(k):
        return tl[0, k] % dblocks

    def keep_of(k):
        return (f_of(k) == f_of(jnp.maximum(k - 1, 0))).astype(jnp.float32)

    def square(h):
        def body(c, acc):
            v = rows_of(xg, c, h)
            xs[c, h * half:(h + 1) * half] = v
            return acc + v * v
        return lax.fori_loop(0, dblocks, body, jnp.zeros((half, blk), jnp.float32), unroll=4)

    acc_own = square(0)
    for d in near:
        remote(carry.at[0], xg.at[1, d], XX + d, XX + d, mate).wait_recv()
    for d in near:
        if d:
            remote(dy_h.at[0], dyg.at[0, d], DYZ + d, DYZ + d, mate).wait_recv()
            go(remote(dyg.at[0, d], dyg.at[1, d], DYX + d, DYX + d, mate))
    acc = jnp.concatenate([acc_own, square(1)], axis=0)
    scale = lax.rsqrt(jnp.sum(acc, axis=-1, keepdims=True) / width + EPS)

    @pl.loop(0, dblocks, unroll=4)
    def _(c):
        cols = pl.ds(pl.multiple_of(c * blk, blk), blk)
        nb[c] = (xs[c] * scale * gv[:, cols]).astype(jnp.bfloat16)

    def g_step(k, cur):
        w = jnp.concatenate([wg[k], wu[k]], axis=1)
        new = jnp.dot(nb[c_of(k)], w, preferred_element_type=jnp.float32)
        cur = cur * keep_of(k) + new
        gu[k] = cur
        return cur
    lax.fori_loop(0, slots, g_step, jnp.zeros((rows, 2 * blk), jnp.float32), unroll=16)

    for f in range(FB_DEV):
        both = gu[last[f]]
        g, u = both[:, :blk], both[:, blk:]
        hb[f] = (g * jax.nn.sigmoid(g) * u).astype(jnp.bfloat16)

    def collect(a):
        @pl.loop(0, dblocks, unroll=4)
        def _(c):
            cols = pl.ds(pl.multiple_of(c * blk, blk), blk)
            total = part[inv[c]]
            for f in range(1, FB_DEV):
                total = total + part[inv[f * dblocks + c]]
            term = total.astype(jnp.bfloat16)
            stage[a, 0, :, cols] = term[:half]
            stage[a, 1, :, cols] = term[half:]

    def o_step(k, _):
        part[k] = jnp.dot(hb[f_of(k)], wd[k], preferred_element_type=jnp.float32)
        return 0
    lax.fori_loop(0, slots, o_step, 0, unroll=16)
    collect(0)
    go(remote(stage.at[0, 1], xr.at[0], FX, FX, mate))

    @pl.loop(0, dblocks, unroll=4)
    def _(c):
        db[c, :half] = rows_of(dyg, c, 0).astype(jnp.bfloat16)

    for d in near:
        remote(dy_h.at[0], dyg.at[1, d], DYX + d, DYX + d, mate).wait_recv()

    @pl.loop(0, dblocks, unroll=4)
    def _(c):
        db[c, half:] = rows_of(dyg, c, 1).astype(jnp.bfloat16)

    def d_step(k, cur):
        new = lax.dot_general(db[c_of(k)], wd[k], NT, preferred_element_type=jnp.float32)
        cur = cur * keep_of(k) + new
        dh[k] = cur
        return cur
    lax.fori_loop(0, slots, d_step, jnp.zeros((rows, blk), jnp.float32), unroll=16)

    for f in range(FB_DEV):
        both = gu[last[f]]
        g, u = both[:, :blk], both[:, blk:]
        sg = jax.nn.sigmoid(g)
        dv = dh[last[f]]
        dgu[f, :, :blk] = (dv * u * sg * (1.0 + g * (1.0 - sg))).astype(jnp.bfloat16)
        dgu[f, :, blk:] = (dv * g * sg).astype(jnp.bfloat16)

    def b_step(k, _):
        w = jnp.concatenate([wg[k], wu[k]], axis=1)
        part[k] = lax.dot_general(dgu[f_of(k)], w, NT, preferred_element_type=jnp.float32)
        return 0
    lax.fori_loop(0, slots, b_step, 0, unroll=16)
    collect(1)
    go(remote(stage.at[1, 1], xr.at[1], BX, BX, mate))

    def pair_sum(a):
        @pl.loop(0, dblocks, unroll=4)
        def _(c):
            cols = pl.ds(pl.multiple_of(c * blk, blk), blk)
            v = stage[a, 0, :, cols].astype(jnp.float32) + xr[a, :, cols].astype(jnp.float32)
            for d in range(line):
                zs[a, d, :, cols] = v[d * per:(d + 1) * per].astype(jnp.bfloat16)

    remote(stage.at[0, 1], xr.at[0], FX, FX, mate).wait_recv()
    pair_sum(0)
    for d in order:
        if d:
            go(remote(zs.at[0, d], zr.at[0, back(d)], FZ + d, FZ + back(d), dev(s, d)))
    remote(stage.at[1, 1], xr.at[1], BX, BX, mate).wait_recv()
    pair_sum(1)
    for d in order:
        go(remote(zs.at[1, d], zr.at[1, back(d)], BZ + d, BZ + back(d), dev(s_prev, d)))

    for d in near:
        if d:
            remote(zs.at[0, d], zr.at[0, d], FZ + d, FZ + d, mate).wait_recv()
    ffn = zs[0, 0].astype(jnp.float32)
    for d in range(1, line):
        ffn = ffn + zr[0, d].astype(jnp.float32)
    for m in range(mb):
        xo = xg[0, 0, m].astype(jnp.float32)
        out[0, m] = (xo + ffn[m * tokd:(m + 1) * tokd]).astype(jnp.bfloat16)

    remote(dy_h.at[0], dyn, DYB, DYB, mate).wait_recv()
    remote(gain, gn, GNB, GNB, mate).wait_recv()
    for d in near:
        remote(zs.at[1, d], zr.at[1, d], BZ + d, BZ + d, mate).wait_recv()
    gnorm = zr[1, 0].astype(jnp.float32)
    for d in range(1, line):
        gnorm = gnorm + zr[1, d].astype(jnp.float32)
    for m in range(mb):
        xo = cown[m].astype(jnp.float32)
        sc = lax.rsqrt(jnp.mean(xo * xo, axis=-1, keepdims=True) + EPS)
        gg = gn[...] * gnorm[m * tokd:(m + 1) * tokd]
        mixed = jnp.mean(xo * gg, axis=-1, keepdims=True)
        gx = dyn[m].astype(jnp.float32) + sc * gg - xo * (sc * sc * sc) * mixed
        gback[0, m] = gx.astype(jnp.bfloat16)
    for c in sent:
        c.wait_send()


def on_device(sections, tensors, carry_in, norm_gain, w_gate, w_up, w_down, tile_list, grad_in):
    _, mb, tokd, width = carry_in.shape
    slots, blk = w_gate.shape[1], w_gate.shape[-1]
    line = tensors // PAIR
    per = mb * tokd
    half = line * per
    rows = PAIR * half
    dblocks = width // blk
    bf, f32 = jnp.bfloat16, jnp.float32
    V = pltpu.VMEM
    anyspec = pl.BlockSpec(memory_space=pl.ANY)
    nsem = 6 * line + 4
    parts = pl.pallas_call(
        functools.partial(kernel, sections, tensors),
        out_shape=[jax.ShapeDtypeStruct(carry_in.shape, bf)] * 2,
        in_specs=[pl.BlockSpec(memory_space=pltpu.SMEM)] + [anyspec] * 6,
        out_specs=[pl.BlockSpec(memory_space=pltpu.VMEM)] * 2,
        scratch_shapes=[
            V((PAIR, line, mb, tokd, width), bf),
            V((PAIR, line, mb, tokd, width), bf),
            V((mb, tokd, width), bf),
            V((1, width), f32),
            V((1, width), f32),
            V((mb, tokd, width), bf),
            V((slots, blk, blk), bf),
            V((slots, blk, blk), bf),
            V((slots, blk, blk), bf),
            V((dblocks, rows, blk), bf),
            V((dblocks, rows, blk), bf),
            V((dblocks, rows, blk), f32),
            V((slots + 1, rows, 2 * blk), f32),
            V((slots + 1, rows, blk), f32),
            V((slots + 1, rows, blk), f32),
            V((FB_DEV, rows, blk), bf),
            V((FB_DEV, rows, 2 * blk), bf),
            V((2, PAIR, half, width), bf),
            V((2, half, width), bf),
            V((2, line, per, width), bf),
            V((2, line, per, width), bf),
            pltpu.SMEM((FB_DEV * dblocks,), jnp.int32),
            pltpu.SMEM((FB_DEV,), jnp.int32),
            pltpu.SemaphoreType.DMA((6,)),
            pltpu.SemaphoreType.DMA((nsem,)),
            pltpu.SemaphoreType.DMA((nsem,)),
        ],
        compiler_params=pltpu.CompilerParams(
            collective_id=0, has_side_effects=True, vmem_limit_bytes=56 * 1024 * 1024
        ),
    )(tile_list, carry_in, norm_gain, w_gate, w_up, w_down, grad_in)
    return pl.pallas_call(
        store,
        out_shape=[jax.ShapeDtypeStruct(carry_in.shape, bf)] * 2,
        in_specs=[pl.BlockSpec(memory_space=pltpu.VMEM)] * 2,
        out_specs=[anyspec] * 2,
        scratch_shapes=[pltpu.SemaphoreType.DMA((2,))],
    )(*parts)


def store(a, b, out_a, out_b, sem):
    copies = [
        pltpu.make_async_copy(a, out_a, sem.at[0]),
        pltpu.make_async_copy(b, out_b, sem.at[1]),
    ]
    for c in copies:
        c.start()
    for c in copies:
        c.wait()


def solution(mesh):
    placed = (
        P("section", None, "tensor", None),
        P("section", None),
        P("section", "tensor", None, None),
        P("section", "tensor", None, None),
        P("section", "tensor", None, None),
        P("section", "tensor"),
        P("section", None, "tensor", None),
    )
    return jax.shard_map(
        functools.partial(on_device, mesh.shape["section"], mesh.shape["tensor"]),
        mesh=mesh,
        in_specs=placed,
        out_specs=(P("section", None, "tensor", None), P("section", None, "tensor", None)),
        check_vma=False,
    )
```

profile of v0, /device:TPU:1, one launch (start us, length us, event | category | flops | bytes accessed | tf_op | source)
XLA Modules:
  0.0 34.3 jit_solution(12760740630077357423)
XLA Ops:
  0.6 32.2 %shard_map.86 = (bf16[1,2,2,4096]{3,2,1,0:T(2,128)(2,1)}, bf16[1,2,2,4096]{3,2,1,0:T(2,128)(2,1)}) custom-call(s32[1,48]{1,0:T(1,128)} %tl.1, bf16[1,2,2,4096]{3,2,1,0:T(2,128)(2,1)} %carry.1, f32[1,4096]{1,0:T(1,128)} %gain.1, bf16[1,48,128,128]{3,2,1,0:T(8,128)(2,1)} %wg_h.1, bf16[1,48,128,128]{3,2,1,0:T(8,128)(2,1)} %wu_h.1, ...), custom_call_target="tpu_custom_call" | custom-call | tf_op jit(solution)/shard_map/pallas_call | solution.py:274
  32.9 1.4 %shard_map.87 = (bf16[1,2,2,4096]{3,2,1,0:T(2,128)(2,1)}, bf16[1,2,2,4096]{3,2,1,0:T(2,128)(2,1)}) custom-call(bf16[1,2,2,4096]{3,2,1,0:T(2,128)(2,1)} %get-tuple-element.4.a, bf16[1,2,2,4096]{3,2,1,0:T(2,128)(2,1)} %get-tuple-element.5.b), custom_call_target="tpu_custom_call" | custom-call | tf_op jit(solution)/shard_map/pallas_call | solution.py:311
where the time goes:
time: 34.5 us; the launch traced here: 34.3 us
  Pallas kernels  33.6 us (97%)
  between operations  0.64 us (2%)
    pallas_call x1, Pallas kernels, on_device(): pl.pallas_call(functools.partial(kernel, sections, tensors), out_shape=[j...  32.2 us
    pallas_call x1, Pallas kernels, on_device(): pl.pallas_call(store, out_shape=[jax.ShapeDtypeStruct(carry_in.shape, bf)...  1.42 us

commit v1 on v0

--- a/solution.py
+++ b/solution.py
@@ -16,10 +16,10 @@
 
 def kernel(
     sections, tensors,
-    tl, carry, gain, wg_h, wu_h, wd_h, dy_h,
+    tl_h, carry, gain, wg_h, wu_h, wd_h, dy_h,
     out, gback,
     xg, dyg, dyn, gn, gv, cown, wg, wu, wd, nb, db, xs, gu, dh, part, hb, dgu,
-    stage, xr, zs, zr, inv, last, lsem, ssem, rsem,
+    stage, xr, zs, zr, tl, inv, last, lsem, ssem, rsem,
 ):
     line = tensors // PAIR
     mb, tokd, width = carry.shape[1:]
@@ -34,56 +34,90 @@
     z, x = t // PAIR, t % PAIR
     s_next, s_prev = (s + 1) % sections, (s + sections - 1) % sections
 
-    def dev(sec, d, other=False):
-        xx = (PAIR - 1 - x) if other else x
-        return (sec, ((z + d) % line) * PAIR + xx)
+    def dev(sec, zt, other=False):
+        return (sec, zt * PAIR + ((PAIR - 1 - x) if other else x))
 
     local = [
-        pltpu.make_async_copy(dy_h.at[0], dyg.at[0, 0], lsem.at[0]),
-        pltpu.make_async_copy(wd_h.at[0], wd, lsem.at[1]),
+        pltpu.make_async_copy(tl_h, tl, lsem.at[6]),
+        pltpu.make_async_copy(carry.at[0], cown, lsem.at[5]),
+        pltpu.make_async_copy(dy_h.at[0], dyg.at[0, z], lsem.at[0]),
+        pltpu.make_async_copy(gain, gv, lsem.at[4]),
         pltpu.make_async_copy(wg_h.at[0], wg, lsem.at[2]),
         pltpu.make_async_copy(wu_h.at[0], wu, lsem.at[3]),
-        pltpu.make_async_copy(gain, gv, lsem.at[4]),
-        pltpu.make_async_copy(carry.at[0], cown, lsem.at[5]),
+        pltpu.make_async_copy(wd_h.at[0], wd, lsem.at[1]),
     ]
     for c in local:
         c.start()
 
+    offsets = sorted((o for o in range(1 - line, line) if o), key=abs)
+
+    def each(offs, body):
+        for o in offs:
+            zt = z + o
+
+            @pl.when(jnp.logical_and(zt >= 0, zt < line))
+            def _(zt=zt):
+                body(zt)
+
     barrier = pltpu.get_barrier_semaphore()
-    friends = [dev(s, d) for d in range(1, line)]
-    friends += [dev(s_next, d) for d in range(line)]
-    friends += [dev(s_prev, d) for d in range(line)]
-    friends += [dev(s, 0, True), dev(s_next, 0, True), dev(s_prev, 0, True)]
-    for f in friends:
-        pl.semaphore_signal(barrier, inc=1, device_id=f, device_id_type=MESH)
-    pl.semaphore_wait(barrier, len(friends))
-
-    def remote(src, dst, ssi, rsi, to):
+
+    def greet(to):
+        pl.semaphore_signal(barrier, inc=1, device_id=to, device_id_type=MESH)
+
+    each(offsets, lambda zt: greet(dev(s, zt)))
+    for zt in range(line):
+        greet(dev(s_next, zt))
+        greet(dev(s_prev, zt))
+    for sec in (s, s_next, s_prev):
+        greet(dev(sec, z, True))
+    pl.semaphore_wait(barrier, (line - 1) + 2 * line + 3)
+
+    def remote(src, dst, si, ri, to):
         return pltpu.make_async_remote_copy(
-            src_ref=src, dst_ref=dst, send_sem=ssem.at[ssi], recv_sem=rsem.at[rsi],
+            src_ref=src, dst_ref=dst, send_sem=ssem.at[si], recv_sem=rsem.at[ri],
             device_id=to, device_id_type=MESH,
         )
 
-    DYZ, XZ, DYX, XX = 0, line, 2 * line, 3 * line
-    FZ, BZ = 4 * line, 5 * line
-    FX, BX, DYB, GNB = 6 * line, 6 * line + 1, 6 * line + 2, 6 * line + 3
-    back = lambda d: (line - d) % line
-    sent = []
-
-    def go(c):
-        c.start()
-        sent.append(c)
-
-    mate = dev(s, 0, True)
-    order = sorted(range(line), key=lambda d: min(d, line - d))
-    for d in order:
-        go(remote(carry.at[0], xg.at[0, back(d)], XZ + d, XZ + back(d), dev(s_next, d)))
-        if d == 0:
-            go(remote(carry.at[0], xg.at[1, 0], XX, XX, dev(s_next, 0, True)))
-    go(remote(dy_h.at[0], dyg.at[1, 0], DYX, DYX, mate))
-    go(remote(dy_h.at[0], dyn, DYB, DYB, dev(s_prev, 0)))
-    go(remote(gain, gn, GNB, GNB, dev(s_prev, 0)))
-
+    XZ, XX, DYZ, DYX, FX, BX, FZ, BZ = (i * line for i in range(8))
+    DYB, GNB = 8 * line, 8 * line + 1
+    mate = dev(s, z, True)
+
+    def x_line(zt):
+        return remote(carry.at[0], xg.at[0, z], XZ + zt, XZ + z, dev(s_next, zt))
+
+    def x_mate():
+        return remote(carry.at[0], xg.at[1, z], XX + z, XX + z, dev(s_next, z, True))
+
+    def x_relay(zt):
+        return remote(xg.at[0, zt], xg.at[1, zt], XX + zt, XX + zt, mate)
+
+    def dy_line(zt):
+        return remote(dy_h.at[0], dyg.at[0, z], DYZ + zt, DYZ + z, dev(s, zt))
+
+    def dy_mate():
+        return remote(dy_h.at[0], dyg.at[1, z], DYX + z, DYX + z, mate)
+
+    def dy_relay(zt):
+        return remote(dyg.at[0, zt], dyg.at[1, zt], DYX + zt, DYX + zt, mate)
+
+    def dy_back():
+        return remote(dy_h.at[0], dyn, DYB, DYB, dev(s_prev, z))
+
+    def gain_back():
+        return remote(gain, gn, GNB, GNB, dev(s_prev, z))
+
+    def got(dst, ri):
+        remote(dst, dst, ri, ri, mate).wait_recv()
+
+    each(offsets, lambda zt: x_line(zt).start())
+    x_line(z).start()
+    x_mate().start()
+    dy_mate().start()
+    each(offsets, lambda zt: dy_line(zt).start())
+    dy_back().start()
+    gain_back().start()
+
+    local[0].wait()
     p = jnp.int32(0)
     for f in range(FB_DEV):
         def cell(i, p, f=f):
@@ -98,17 +132,6 @@
     dh[slots] = jnp.zeros((rows, blk), jnp.float32)
     part[slots] = jnp.zeros((rows, blk), jnp.float32)
 
-    near = sorted(range(line), key=lambda d: min(d, line - d))
-    for d in near:
-        remote(carry.at[0], xg.at[0, d], XZ + d, XZ + d, mate).wait_recv()
-        if d:
-            go(remote(xg.at[0, d], xg.at[1, d], XX + d, XX + d, mate))
-    for d in order:
-        if d:
-            go(remote(dy_h.at[0], dyg.at[0, back(d)], DYZ + d, DYZ + back(d), dev(s, d)))
-    for c in local:
-        c.wait()
-
     def rows_of(ref, c, h):
         cols = pl.ds(pl.multiple_of(c * blk, blk), blk)
         pieces = []
@@ -133,13 +156,26 @@
             return acc + v * v
         return lax.fori_loop(0, dblocks, body, jnp.zeros((half, blk), jnp.float32), unroll=4)
 
+    def pack_dy(h):
+        @pl.loop(0, dblocks, unroll=4)
+        def _(c):
+            db[c, h * half:(h + 1) * half] = rows_of(dyg, c, h).astype(jnp.bfloat16)
+
+    def relay_x(zt):
+        got(xg.at[0, zt], XZ + zt)
+        x_relay(zt).start()
+    each(offsets, relay_x)
+    got(xg.at[0, z], XZ + z)
     acc_own = square(0)
-    for d in near:
-        remote(carry.at[0], xg.at[1, d], XX + d, XX + d, mate).wait_recv()
-    for d in near:
-        if d:
-            remote(dy_h.at[0], dyg.at[0, d], DYZ + d, DYZ + d, mate).wait_recv()
-            go(remote(dyg.at[0, d], dyg.at[1, d], DYX + d, DYX + d, mate))
+    def relay_dy(zt):
+        got(dyg.at[0, zt], DYZ + zt)
+        dy_relay(zt).start()
+    each(offsets, relay_dy)
+    for c in local[1:]:
+        c.wait()
+    pack_dy(0)
+    for zt in range(line):
+        got(xg.at[1, zt], XX + zt)
     acc = jnp.concatenate([acc_own, square(1)], axis=0)
     scale = lax.rsqrt(jnp.sum(acc, axis=-1, keepdims=True) / width + EPS)
 
@@ -168,27 +204,33 @@
             total = part[inv[c]]
             for f in range(1, FB_DEV):
                 total = total + part[inv[f * dblocks + c]]
-            term = total.astype(jnp.bfloat16)
-            stage[a, 0, :, cols] = term[:half]
-            stage[a, 1, :, cols] = term[half:]
+            for h in range(PAIR):
+                for d in range(line):
+                    r = (h * line + d) * per
+                    stage[a, h, d, :, cols] = total[r:r + per].astype(jnp.bfloat16)
+
+    chunks = sorted(range(line), key=lambda d: min(2 * d, 2 * (line - 1 - d) + 1))
+
+    def swap(a, base, zt):
+        return remote(stage.at[a, 1, zt], xr.at[a, zt], base + zt, base + zt, mate)
+
+    def f_out(zt):
+        return remote(zs.at[0, zt], zr.at[0, z], FZ + zt, FZ + z, dev(s, zt))
+
+    def b_out(zt):
+        return remote(zs.at[1, zt], zr.at[1, z], BZ + zt, BZ + z, dev(s_prev, zt))
 
     def o_step(k, _):
         part[k] = jnp.dot(hb[f_of(k)], wd[k], preferred_element_type=jnp.float32)
         return 0
     lax.fori_loop(0, slots, o_step, 0, unroll=16)
     collect(0)
-    go(remote(stage.at[0, 1], xr.at[0], FX, FX, mate))
-
-    @pl.loop(0, dblocks, unroll=4)
-    def _(c):
-        db[c, :half] = rows_of(dyg, c, 0).astype(jnp.bfloat16)
-
-    for d in near:
-        remote(dy_h.at[0], dyg.at[1, d], DYX + d, DYX + d, mate).wait_recv()
-
-    @pl.loop(0, dblocks, unroll=4)
-    def _(c):
-        db[c, half:] = rows_of(dyg, c, 1).astype(jnp.bfloat16)
+    for zt in chunks:
+        swap(0, FX, zt).start()
+
+    for zt in range(line):
+        got(dyg.at[1, zt], DYX + zt)
+    pack_dy(1)
 
     def d_step(k, cur):
         new = lax.dot_general(db[c_of(k)], wd[k], NT, preferred_element_type=jnp.float32)
@@ -211,40 +253,50 @@
         return 0
     lax.fori_loop(0, slots, b_step, 0, unroll=16)
     collect(1)
-    go(remote(stage.at[1, 1], xr.at[1], BX, BX, mate))
-
-    def pair_sum(a):
-        @pl.loop(0, dblocks, unroll=4)
-        def _(c):
-            cols = pl.ds(pl.multiple_of(c * blk, blk), blk)
-            v = stage[a, 0, :, cols].astype(jnp.float32) + xr[a, :, cols].astype(jnp.float32)
-            for d in range(line):
-                zs[a, d, :, cols] = v[d * per:(d + 1) * per].astype(jnp.bfloat16)
-
-    remote(stage.at[0, 1], xr.at[0], FX, FX, mate).wait_recv()
-    pair_sum(0)
-    for d in order:
-        if d:
-            go(remote(zs.at[0, d], zr.at[0, back(d)], FZ + d, FZ + back(d), dev(s, d)))
-    remote(stage.at[1, 1], xr.at[1], BX, BX, mate).wait_recv()
-    pair_sum(1)
-    for d in order:
-        go(remote(zs.at[1, d], zr.at[1, back(d)], BZ + d, BZ + back(d), dev(s_prev, d)))
-
-    for d in near:
-        if d:
-            remote(zs.at[0, d], zr.at[0, d], FZ + d, FZ + d, mate).wait_recv()
-    ffn = zs[0, 0].astype(jnp.float32)
+    for zt in chunks:
+        swap(1, BX, zt).start()
+
+    def pair_sum(a, zt):
+        return stage[a, 0, zt].astype(jnp.float32) + xr[a, zt].astype(jnp.float32)
+
+    for zt in chunks:
+        got(xr.at[0, zt], FX + zt)
+        zs[0, zt] = pair_sum(0, zt).astype(jnp.bfloat16)
+
+        @pl.when(z != zt)
+        def _(zt=zt):
+            f_out(zt).start()
+    for zt in chunks:
+        got(xr.at[1, zt], BX + zt)
+        zs[1, zt] = pair_sum(1, zt).astype(jnp.bfloat16)
+        b_out(zt).start()
+
+    zr[0, z] = zs[0, z]
+    each(offsets, lambda zt: got(zr.at[0, zt], FZ + zt))
+    ffn = zr[0, 0].astype(jnp.float32)
     for d in range(1, line):
         ffn = ffn + zr[0, d].astype(jnp.float32)
     for m in range(mb):
-        xo = xg[0, 0, m].astype(jnp.float32)
+        xo = xg[0, z, m].astype(jnp.float32)
         out[0, m] = (xo + ffn[m * tokd:(m + 1) * tokd]).astype(jnp.bfloat16)
 
-    remote(dy_h.at[0], dyn, DYB, DYB, mate).wait_recv()
-    remote(gain, gn, GNB, GNB, mate).wait_recv()
-    for d in near:
-        remote(zs.at[1, d], zr.at[1, d], BZ + d, BZ + d, mate).wait_recv()
+    each(offsets, lambda zt: x_line(zt).wait_send())
+    x_line(z).wait_send()
+    x_mate().wait_send()
+    each(offsets, lambda zt: x_relay(zt).wait_send())
+    dy_mate().wait_send()
+    each(offsets, lambda zt: dy_line(zt).wait_send())
+    each(offsets, lambda zt: dy_relay(zt).wait_send())
+    dy_back().wait_send()
+    gain_back().wait_send()
+    for zt in range(line):
+        swap(0, FX, zt).wait_send()
+        swap(1, BX, zt).wait_send()
+    each(offsets, lambda zt: f_out(zt).wait_send())
+    got(dyn, DYB)
+    got(gn, GNB)
+    for zt in range(line):
+        got(zr.at[1, zt], BZ + zt)
     gnorm = zr[1, 0].astype(jnp.float32)
     for d in range(1, line):
         gnorm = gnorm + zr[1, d].astype(jnp.float32)
@@ -255,8 +307,8 @@
         mixed = jnp.mean(xo * gg, axis=-1, keepdims=True)
         gx = dyn[m].astype(jnp.float32) + sc * gg - xo * (sc * sc * sc) * mixed
         gback[0, m] = gx.astype(jnp.bfloat16)
-    for c in sent:
-        c.wait_send()
+    for zt in range(line):
+        b_out(zt).wait_send()
 
 
 def on_device(sections, tensors, carry_in, norm_gain, w_gate, w_up, w_down, tile_list, grad_in):
@@ -270,11 +322,11 @@
     bf, f32 = jnp.bfloat16, jnp.float32
     V = pltpu.VMEM
     anyspec = pl.BlockSpec(memory_space=pl.ANY)
-    nsem = 6 * line + 4
+    nsem = 8 * line + 2
     parts = pl.pallas_call(
         functools.partial(kernel, sections, tensors),
         out_shape=[jax.ShapeDtypeStruct(carry_in.shape, bf)] * 2,
-        in_specs=[pl.BlockSpec(memory_space=pltpu.SMEM)] + [anyspec] * 6,
+        in_specs=[anyspec] * 7,
         out_specs=[pl.BlockSpec(memory_space=pltpu.VMEM)] * 2,
         scratch_shapes=[
             V((PAIR, line, mb, tokd, width), bf),
@@ -294,13 +346,14 @@
             V((slots + 1, rows, blk), f32),
             V((FB_DEV, rows, blk), bf),
             V((FB_DEV, rows, 2 * blk), bf),
-            V((2, PAIR, half, width), bf),
-            V((2, half, width), bf),
+            V((2, PAIR, line, per, width), bf),
             V((2, line, per, width), bf),
             V((2, line, per, width), bf),
+            V((2, line, per, width), bf),
+            pltpu.SMEM((1, slots), jnp.int32),
             pltpu.SMEM((FB_DEV * dblocks,), jnp.int32),
             pltpu.SMEM((FB_DEV,), jnp.int32),
-            pltpu.SemaphoreType.DMA((6,)),
+            pltpu.SemaphoreType.DMA((7,)),
             pltpu.SemaphoreType.DMA((nsem,)),
             pltpu.SemaphoreType.DMA((nsem,)),
         ],

time: 34.5 us -> 30.5 us (0.88)
  Pallas kernels: 33.6 us -> 29.6 us
    pallas_call x1, Pallas kernels: 32.2 us -> 28.2 us  [on_device(): pl.pallas_call(functools.partial(kernel, sections, tensors), out_shape=[j...]
where the time goes in v1:
time: 30.5 us; the launch traced here: 30.3 us
  Pallas kernels  29.6 us (97%)
  between operations  0.64 us (2%)
    pallas_call x1, Pallas kernels, on_device(): pl.pallas_call(functools.partial(kernel, sections, tensors), out_shape=[j...  28.2 us
    pallas_call x1, Pallas kernels, on_device(): pl.pallas_call(store, out_shape=[jax.ShapeDtypeStruct(carry_in.shape, bf)...  1.42 us

profile of v1, /device:TPU:1, one launch (start us, length us, event | category | flops | bytes accessed | tf_op | source)
XLA Modules:
  0.0 30.3 jit_solution(7666914117579356004)
XLA Ops:
  0.6 28.2 %shard_map.86 = (bf16[1,2,2,4096]{3,2,1,0:T(2,128)(2,1)}, bf16[1,2,2,4096]{3,2,1,0:T(2,128)(2,1)}) custom-call(s32[1,48]{1,0:T(1,128)} %tl_h.1, bf16[1,2,2,4096]{3,2,1,0:T(2,128)(2,1)} %carry.1, f32[1,4096]{1,0:T(1,128)} %gain.1, bf16[1,48,128,128]{3,2,1,0:T(8,128)(2,1)} %wg_h.1, bf16[1,48,128,128]{3,2,1,0:T(8,128)(2,1)} %wu_h.1, ...), custom_call_target="tpu_custom_call" | custom-call | tf_op jit(solution)/shard_map/pallas_call | solution.py:326
  28.9 1.4 %shard_map.87 = (bf16[1,2,2,4096]{3,2,1,0:T(2,128)(2,1)}, bf16[1,2,2,4096]{3,2,1,0:T(2,128)(2,1)}) custom-call(bf16[1,2,2,4096]{3,2,1,0:T(2,128)(2,1)} %get-tuple-element.4.a, bf16[1,2,2,4096]{3,2,1,0:T(2,128)(2,1)} %get-tuple-element.5.b), custom_call_target="tpu_custom_call" | custom-call | tf_op jit(solution)/shard_map/pallas_call | solution.py:364

commit v2 on v1

--- a/solution.py
+++ b/solution.py
@@ -190,7 +190,7 @@
         cur = cur * keep_of(k) + new
         gu[k] = cur
         return cur
-    lax.fori_loop(0, slots, g_step, jnp.zeros((rows, 2 * blk), jnp.float32), unroll=16)
+    lax.fori_loop(0, slots, g_step, jnp.zeros((rows, 2 * blk), jnp.float32), unroll=slots)
 
     for f in range(FB_DEV):
         both = gu[last[f]]
@@ -223,7 +223,7 @@
     def o_step(k, _):
         part[k] = jnp.dot(hb[f_of(k)], wd[k], preferred_element_type=jnp.float32)
         return 0
-    lax.fori_loop(0, slots, o_step, 0, unroll=16)
+    lax.fori_loop(0, slots, o_step, 0, unroll=slots)
     collect(0)
     for zt in chunks:
         swap(0, FX, zt).start()
@@ -237,7 +237,7 @@
         cur = cur * keep_of(k) + new
         dh[k] = cur
         return cur
-    lax.fori_loop(0, slots, d_step, jnp.zeros((rows, blk), jnp.float32), unroll=16)
+    lax.fori_loop(0, slots, d_step, jnp.zeros((rows, blk), jnp.float32), unroll=slots)
 
     for f in range(FB_DEV):
         both = gu[last[f]]
@@ -251,7 +251,7 @@
         w = jnp.concatenate([wg[k], wu[k]], axis=1)
         part[k] = lax.dot_general(dgu[f_of(k)], w, NT, preferred_element_type=jnp.float32)
         return 0
-    lax.fori_loop(0, slots, b_step, 0, unroll=16)
+    lax.fori_loop(0, slots, b_step, 0, unroll=slots)
     collect(1)
     for zt in chunks:
         swap(1, BX, zt).start()
@@ -326,7 +326,7 @@
     parts = pl.pallas_call(
         functools.partial(kernel, sections, tensors),
         out_shape=[jax.ShapeDtypeStruct(carry_in.shape, bf)] * 2,
-        in_specs=[anyspec] * 7,
+        in_specs=[pl.BlockSpec(memory_space=pltpu.HBM)] * 7,
         out_specs=[pl.BlockSpec(memory_space=pltpu.VMEM)] * 2,
         scratch_shapes=[
             V((PAIR, line, mb, tokd, width), bf),
@@ -358,15 +358,16 @@
             pltpu.SemaphoreType.DMA((nsem,)),
         ],
         compiler_params=pltpu.CompilerParams(
-            collective_id=0, has_side_effects=True, vmem_limit_bytes=56 * 1024 * 1024
+            collective_id=0, has_side_effects=True, vmem_limit_bytes=48 * 1024 * 1024
         ),
-    )(tile_list, carry_in, norm_gain, w_gate, w_up, w_down, grad_in)
+    )(*(pltpu.with_memory_space_constraint(v, pltpu.HBM) for v in (tile_list, carry_in, norm_gain, w_gate, w_up, w_down, grad_in)))
     return pl.pallas_call(
         store,
         out_shape=[jax.ShapeDtypeStruct(carry_in.shape, bf)] * 2,
         in_specs=[pl.BlockSpec(memory_space=pltpu.VMEM)] * 2,
         out_specs=[anyspec] * 2,
         scratch_shapes=[pltpu.SemaphoreType.DMA((2,))],
+        compiler_params=pltpu.CompilerParams(vmem_limit_bytes=1024 * 1024),
     )(*parts)
 
 

time: 30.5 us -> 28.4 us (0.931)
  Pallas kernels: 29.6 us -> 27.6 us
    pallas_call x1, Pallas kernels: 28.2 us -> 26.9 us  [on_device(): pl.pallas_call(functools.partial(kernel, sections, tensors), out_shape=[j...]
    pallas_call x1, Pallas kernels: 1.42 us -> 0.65 us  [on_device(): pl.pallas_call(store, out_shape=[jax.ShapeDtypeStruct(carry_in.shape, bf)...]
where the time goes in v2:
time: 28.4 us; the launch traced here: 28.2 us
  Pallas kernels  27.6 us (97%)
  between operations  0.64 us (2%)
    pallas_call x1, Pallas kernels, on_device(): pl.pallas_call(functools.partial(kernel, sections, tensors), out_shape=[j...  26.9 us
    pallas_call x1, Pallas kernels, on_device(): pl.pallas_call(store, out_shape=[jax.ShapeDtypeStruct(carry_in.shape, bf)...  0.65 us

profile of v2, /device:TPU:1, one launch (start us, length us, event | category | flops | bytes accessed | tf_op | source)
XLA Modules:
  0.0 28.2 jit_solution(4337699596999853078)
XLA Ops:
  0.6 26.9 %shard_map.86 = (bf16[1,2,2,4096]{3,2,1,0:T(2,128)(2,1)S(1)}, bf16[1,2,2,4096]{3,2,1,0:T(2,128)(2,1)S(1)}) custom-call(s32[1,48]{1,0:T(1,128)} %tl_h.1, bf16[1,2,2,4096]{3,2,1,0:T(2,128)(2,1)} %carry.1, f32[1,4096]{1,0:T(1,128)} %gain.1, bf16[1,48,128,128]{3,2,1,0:T(8,128)(2,1)} %wg_h.1, bf16[1,48,128,128]{3,2,1,0:T(8,128)(2,1)} %wu_h.1, ...), custom_call_target="tpu_custom_call" | custom-call | tf_op jit(solution)/shard_map/pallas_call | solution.py:326
  27.6 0.6 %shard_map.87 = (bf16[1,2,2,4096]{3,2,1,0:T(2,128)(2,1)}, bf16[1,2,2,4096]{3,2,1,0:T(2,128)(2,1)}) custom-call(bf16[1,2,2,4096]{3,2,1,0:T(2,128)(2,1)S(1)} %get-tuple-element.4.a, bf16[1,2,2,4096]{3,2,1,0:T(2,128)(2,1)S(1)} %get-tuple-element.5.b), custom_call_target="tpu_custom_call" | custom-call | tf_op jit(solution)/shard_map/pallas_call | solution.py:364

commit v3 on v2

--- a/solution.py
+++ b/solution.py
@@ -11,7 +11,6 @@
 EPS = 1e-05
 PAIR = 2
 MESH = pl.DeviceIdType.MESH
-NT = (((1,), (1,)), ((), ()))
 
 
 def kernel(
@@ -19,7 +18,7 @@
     tl_h, carry, gain, wg_h, wu_h, wd_h, dy_h,
     out, gback,
     xg, dyg, dyn, gn, gv, cown, wg, wu, wd, nb, db, xs, gu, dh, part, hb, dgu,
-    stage, xr, zs, zr, tl, inv, last, lsem, ssem, rsem,
+    stage, xr, zs, zr, wr, gsum, wdt, wgt, tl, inv, last, lsem, ssem, rsem,
 ):
     line = tensors // PAIR
     mb, tokd, width = carry.shape[1:]
@@ -64,13 +63,15 @@
     def greet(to):
         pl.semaphore_signal(barrier, inc=1, device_id=to, device_id_type=MESH)
 
-    each(offsets, lambda zt: greet(dev(s, zt)))
-    for zt in range(line):
-        greet(dev(s_next, zt))
+    greet(dev(s, z, True))
+    greet(dev(s_prev, z))
+    greet(dev(s_prev, z, True))
+
+    def greet_line(zt):
+        greet(dev(s, zt))
         greet(dev(s_prev, zt))
-    for sec in (s, s_next, s_prev):
-        greet(dev(sec, z, True))
-    pl.semaphore_wait(barrier, (line - 1) + 2 * line + 3)
+    each(offsets, greet_line)
+    pl.semaphore_wait(barrier, 2 * line + 1)
 
     def remote(src, dst, si, ri, to):
         return pltpu.make_async_remote_copy(
@@ -79,7 +80,8 @@
         )
 
     XZ, XX, DYZ, DYX, FX, BX, FZ, BZ = (i * line for i in range(8))
-    DYB, GNB = 8 * line, 8 * line + 1
+    BW = 8 * line
+    DYB, GNB = 9 * line, 9 * line + 1
     mate = dev(s, z, True)
 
     def x_line(zt):
@@ -113,9 +115,6 @@
     x_line(z).start()
     x_mate().start()
     dy_mate().start()
-    each(offsets, lambda zt: dy_line(zt).start())
-    dy_back().start()
-    gain_back().start()
 
     local[0].wait()
     p = jnp.int32(0)
@@ -161,17 +160,28 @@
         def _(c):
             db[c, h * half:(h + 1) * half] = rows_of(dyg, c, h).astype(jnp.bfloat16)
 
+    def turn(ref, src, at):
+        @pl.loop(0, slots, unroll=8)
+        def _(k):
+            ref[k, at:at + blk] = src[k].T
+
+    each(offsets, lambda zt: dy_line(zt).start())
+    for i, (ref, src, at) in ((6, (wdt, wd, 0)), (4, (wgt, wg, 0)), (5, (wgt, wu, blk))):
+        local[i].wait()
+        turn(ref, src, at)
     def relay_x(zt):
         got(xg.at[0, zt], XZ + zt)
         x_relay(zt).start()
     each(offsets, relay_x)
     got(xg.at[0, z], XZ + z)
+    dy_back().start()
+    gain_back().start()
     acc_own = square(0)
     def relay_dy(zt):
         got(dyg.at[0, zt], DYZ + zt)
         dy_relay(zt).start()
     each(offsets, relay_dy)
-    for c in local[1:]:
+    for c in local[1:4]:
         c.wait()
     pack_dy(0)
     for zt in range(line):
@@ -220,6 +230,15 @@
     def b_out(zt):
         return remote(zs.at[1, zt], zr.at[1, z], BZ + zt, BZ + z, dev(s_prev, zt))
 
+    ends = []
+    inner = [zt for zt in chunks if zt not in ends]
+
+    def b_own(zt):
+        return remote(stage.at[1, 0, zt], zr.at[1, z], BZ + zt, BZ + z, dev(s_prev, zt))
+
+    def b_other(zt):
+        return remote(stage.at[1, 1, zt], wr.at[z], BW + zt, BW + z, dev(s_prev, zt, True))
+
     def o_step(k, _):
         part[k] = jnp.dot(hb[f_of(k)], wd[k], preferred_element_type=jnp.float32)
         return 0
@@ -233,7 +252,7 @@
     pack_dy(1)
 
     def d_step(k, cur):
-        new = lax.dot_general(db[c_of(k)], wd[k], NT, preferred_element_type=jnp.float32)
+        new = jnp.dot(db[c_of(k)], wdt[k], preferred_element_type=jnp.float32)
         cur = cur * keep_of(k) + new
         dh[k] = cur
         return cur
@@ -248,8 +267,7 @@
         dgu[f, :, blk:] = (dv * g * sg).astype(jnp.bfloat16)
 
     def b_step(k, _):
-        w = jnp.concatenate([wg[k], wu[k]], axis=1)
-        part[k] = lax.dot_general(dgu[f_of(k)], w, NT, preferred_element_type=jnp.float32)
+        part[k] = jnp.dot(dgu[f_of(k)], wgt[k], preferred_element_type=jnp.float32)
         return 0
     lax.fori_loop(0, slots, b_step, 0, unroll=slots)
     collect(1)
@@ -266,7 +284,7 @@
         @pl.when(z != zt)
         def _(zt=zt):
             f_out(zt).start()
-    for zt in chunks:
+    for zt in inner:
         got(xr.at[1, zt], BX + zt)
         zs[1, zt] = pair_sum(1, zt).astype(jnp.bfloat16)
         b_out(zt).start()
@@ -291,15 +309,30 @@
     gain_back().wait_send()
     for zt in range(line):
         swap(0, FX, zt).wait_send()
+    for zt in inner:
         swap(1, BX, zt).wait_send()
+    for zt in ends:
+        b_own(zt).wait_send()
+        b_other(zt).wait_send()
     each(offsets, lambda zt: f_out(zt).wait_send())
     got(dyn, DYB)
     got(gn, GNB)
     for zt in range(line):
         got(zr.at[1, zt], BZ + zt)
-    gnorm = zr[1, 0].astype(jnp.float32)
+    total = zr[1, 0].astype(jnp.float32)
     for d in range(1, line):
-        gnorm = gnorm + zr[1, d].astype(jnp.float32)
+        total = total + zr[1, d].astype(jnp.float32)
+    gsum[...] = total
+
+    @pl.when(z < 0)
+    def _():
+        for zt in range(line):
+            got(wr.at[zt], BW + zt)
+        total = gsum[...]
+        for d in range(line):
+            total = total + wr[d].astype(jnp.float32)
+        gsum[...] = total
+    gnorm = gsum[...]
     for m in range(mb):
         xo = cown[m].astype(jnp.float32)
         sc = lax.rsqrt(jnp.mean(xo * xo, axis=-1, keepdims=True) + EPS)
@@ -307,7 +340,7 @@
         mixed = jnp.mean(xo * gg, axis=-1, keepdims=True)
         gx = dyn[m].astype(jnp.float32) + sc * gg - xo * (sc * sc * sc) * mixed
         gback[0, m] = gx.astype(jnp.bfloat16)
-    for zt in range(line):
+    for zt in inner:
         b_out(zt).wait_send()
 
 
@@ -322,7 +355,7 @@
     bf, f32 = jnp.bfloat16, jnp.float32
     V = pltpu.VMEM
     anyspec = pl.BlockSpec(memory_space=pl.ANY)
-    nsem = 8 * line + 2
+    nsem = 9 * line + 2
     parts = pl.pallas_call(
         functools.partial(kernel, sections, tensors),
         out_shape=[jax.ShapeDtypeStruct(carry_in.shape, bf)] * 2,
@@ -350,6 +383,10 @@
             V((2, line, per, width), bf),
             V((2, line, per, width), bf),
             V((2, line, per, width), bf),
+            V((line, per, width), bf),
+            V((per, width), f32),
+            V((slots, blk, blk), bf),
+            V((slots, 2 * blk, blk), bf),
             pltpu.SMEM((1, slots), jnp.int32),
             pltpu.SMEM((FB_DEV * dblocks,), jnp.int32),
             pltpu.SMEM((FB_DEV,), jnp.int32),

time: 28.4 us -> 28.4 us (level)
  no operation moved by 1% of the time
where the time goes in v3:
time: 28.4 us; the launch traced here: 28.3 us
  Pallas kernels  27.6 us (97%)
  between operations  0.64 us (2%)
    pallas_call x1, Pallas kernels, on_device(): pl.pallas_call(functools.partial(kernel, sections, tensors), out_shape=[j...  27 us
    pallas_call x1, Pallas kernels, on_device(): pl.pallas_call(store, out_shape=[jax.ShapeDtypeStruct(carry_in.shape, bf)...  0.65 us

profile of v3, /device:TPU:1, one launch (start us, length us, event | category | flops | bytes accessed | tf_op | source)
XLA Modules:
  0.0 28.3 jit_solution(2067536363162417413)
XLA Ops:
  0.6 27.0 %shard_map.86 = (bf16[1,2,2,4096]{3,2,1,0:T(2,128)(2,1)S(1)}, bf16[1,2,2,4096]{3,2,1,0:T(2,128)(2,1)S(1)}) custom-call(s32[1,48]{1,0:T(1,128)} %tl_h.1, bf16[1,2,2,4096]{3,2,1,0:T(2,128)(2,1)} %carry.1, f32[1,4096]{1,0:T(1,128)} %gain.1, bf16[1,48,128,128]{3,2,1,0:T(8,128)(2,1)} %wg_h.1, bf16[1,48,128,128]{3,2,1,0:T(8,128)(2,1)} %wu_h.1, ...), custom_call_target="tpu_custom_call" | custom-call | tf_op jit(solution)/shard_map/pallas_call | solution.py:359
  27.6 0.6 %shard_map.87 = (bf16[1,2,2,4096]{3,2,1,0:T(2,128)(2,1)}, bf16[1,2,2,4096]{3,2,1,0:T(2,128)(2,1)}) custom-call(bf16[1,2,2,4096]{3,2,1,0:T(2,128)(2,1)S(1)} %get-tuple-element.4.a, bf16[1,2,2,4096]{3,2,1,0:T(2,128)(2,1)S(1)} %get-tuple-element.5.b), custom_call_target="tpu_custom_call" | custom-call | tf_op jit(solution)/shard_map/pallas_call | solution.py:401

commit v4 on v3

--- a/solution.py
+++ b/solution.py
@@ -18,7 +18,7 @@
     tl_h, carry, gain, wg_h, wu_h, wd_h, dy_h,
     out, gback,
     xg, dyg, dyn, gn, gv, cown, wg, wu, wd, nb, db, xs, gu, dh, part, hb, dgu,
-    stage, xr, zs, zr, wr, gsum, wdt, wgt, tl, inv, last, lsem, ssem, rsem,
+    stage, xr, zs, zr, wdt, wgt, tl, inv, last, lsem, ssem, rsem,
 ):
     line = tensors // PAIR
     mb, tokd, width = carry.shape[1:]
@@ -79,37 +79,40 @@
             device_id=to, device_id_type=MESH,
         )
 
-    XZ, XX, DYZ, DYX, FX, BX, FZ, BZ = (i * line for i in range(8))
-    BW = 8 * line
-    DYB, GNB = 9 * line, 9 * line + 1
+    XZ, DYZ, FX, BX, FZ = (i * line for i in range(5))
+    XX, DYX, BZ, DYB, GNB = (5 * line + i for i in range(5))
+    SX, SDY, SW, SB, SG, SF = range(6)
     mate = dev(s, z, True)
 
     def x_line(zt):
-        return remote(carry.at[0], xg.at[0, z], XZ + zt, XZ + z, dev(s_next, zt))
+        return remote(carry.at[0], xg.at[0, z], SX, XZ + z, dev(s_next, zt))
 
     def x_mate():
-        return remote(carry.at[0], xg.at[1, z], XX + z, XX + z, dev(s_next, z, True))
+        return remote(carry.at[0], xg.at[1, z], SX, XX, dev(s_next, z, True))
 
     def x_relay(zt):
-        return remote(xg.at[0, zt], xg.at[1, zt], XX + zt, XX + zt, mate)
+        return remote(xg.at[0, zt], xg.at[1, zt], SX, XX, mate)
 
     def dy_line(zt):
-        return remote(dy_h.at[0], dyg.at[0, z], DYZ + zt, DYZ + z, dev(s, zt))
+        return remote(dy_h.at[0], dyg.at[0, z], SDY, DYZ + z, dev(s, zt))
 
     def dy_mate():
-        return remote(dy_h.at[0], dyg.at[1, z], DYX + z, DYX + z, mate)
+        return remote(dy_h.at[0], dyg.at[1, z], SDY, DYX, mate)
 
     def dy_relay(zt):
-        return remote(dyg.at[0, zt], dyg.at[1, zt], DYX + zt, DYX + zt, mate)
+        return remote(dyg.at[0, zt], dyg.at[1, zt], SDY, DYX, mate)
 
     def dy_back():
-        return remote(dy_h.at[0], dyn, DYB, DYB, dev(s_prev, z))
+        return remote(dy_h.at[0], dyn, SDY, DYB, dev(s_prev, z))
 
     def gain_back():
-        return remote(gain, gn, GNB, GNB, dev(s_prev, z))
+        return remote(gain, gn, SG, GNB, dev(s_prev, z))
 
     def got(dst, ri):
-        remote(dst, dst, ri, ri, mate).wait_recv()
+        remote(dst, dst, 0, ri, mate).wait_recv()
+
+    def gone(src, si):
+        remote(src, src, si, 0, mate).wait_send()
 
     each(offsets, lambda zt: x_line(zt).start())
     x_line(z).start()
@@ -184,8 +187,7 @@
     for c in local[1:4]:
         c.wait()
     pack_dy(0)
-    for zt in range(line):
-        got(xg.at[1, zt], XX + zt)
+    got(xg.at[1], XX)
     acc = jnp.concatenate([acc_own, square(1)], axis=0)
     scale = lax.rsqrt(jnp.sum(acc, axis=-1, keepdims=True) / width + EPS)
 
@@ -219,36 +221,44 @@
                     r = (h * line + d) * per
                     stage[a, h, d, :, cols] = total[r:r + per].astype(jnp.bfloat16)
 
-    chunks = sorted(range(line), key=lambda d: min(2 * d, 2 * (line - 1 - d) + 1))
+    def away(body):
+        @pl.when(2 * z < line)
+        def _():
+            for zt in reversed(range(line)):
+                @pl.when(z != zt)
+                def _(zt=zt):
+                    body(zt)
+
+        @pl.when(2 * z >= line)
+        def _():
+            for zt in range(line):
+                @pl.when(z != zt)
+                def _(zt=zt):
+                    body(zt)
+
+    def own(body):
+        for zt in range(line):
+            @pl.when(z == zt)
+            def _(zt=zt):
+                body(zt)
 
     def swap(a, base, zt):
-        return remote(stage.at[a, 1, zt], xr.at[a, zt], base + zt, base + zt, mate)
+        return remote(stage.at[a, 1, zt], xr.at[a, zt], SW, base + zt, mate)
 
     def f_out(zt):
-        return remote(zs.at[0, zt], zr.at[0, z], FZ + zt, FZ + z, dev(s, zt))
+        return remote(zs.at[0, zt], zr.at[0, z], SF + zt, FZ + z, dev(s, zt))
 
     def b_out(zt):
-        return remote(zs.at[1, zt], zr.at[1, z], BZ + zt, BZ + z, dev(s_prev, zt))
-
-    ends = []
-    inner = [zt for zt in chunks if zt not in ends]
-
-    def b_own(zt):
-        return remote(stage.at[1, 0, zt], zr.at[1, z], BZ + zt, BZ + z, dev(s_prev, zt))
-
-    def b_other(zt):
-        return remote(stage.at[1, 1, zt], wr.at[z], BW + zt, BW + z, dev(s_prev, zt, True))
+        return remote(zs.at[1, zt], zr.at[1, z], SB, BZ, dev(s_prev, zt))
 
     def o_step(k, _):
         part[k] = jnp.dot(hb[f_of(k)], wd[k], preferred_element_type=jnp.float32)
         return 0
     lax.fori_loop(0, slots, o_step, 0, unroll=slots)
     collect(0)
-    for zt in chunks:
-        swap(0, FX, zt).start()
-
-    for zt in range(line):
-        got(dyg.at[1, zt], DYX + zt)
+    away(lambda zt: swap(0, FX, zt).start())
+
+    got(dyg.at[1], DYX)
     pack_dy(1)
 
     def d_step(k, cur):
@@ -271,25 +281,28 @@
         return 0
     lax.fori_loop(0, slots, b_step, 0, unroll=slots)
     collect(1)
-    for zt in chunks:
-        swap(1, BX, zt).start()
+    away(lambda zt: swap(1, BX, zt).start())
+    swap(1, BX, z).start()
+    swap(0, FX, z).start()
 
     def pair_sum(a, zt):
         return stage[a, 0, zt].astype(jnp.float32) + xr[a, zt].astype(jnp.float32)
 
-    for zt in chunks:
+    def f_send(zt):
         got(xr.at[0, zt], FX + zt)
         zs[0, zt] = pair_sum(0, zt).astype(jnp.bfloat16)
-
-        @pl.when(z != zt)
-        def _(zt=zt):
-            f_out(zt).start()
-    for zt in inner:
+        f_out(zt).start()
+    away(f_send)
+    def b_send(zt):
         got(xr.at[1, zt], BX + zt)
         zs[1, zt] = pair_sum(1, zt).astype(jnp.bfloat16)
         b_out(zt).start()
-
-    zr[0, z] = zs[0, z]
+    away(b_send)
+    own(b_send)
+    def f_keep(zt):
+        got(xr.at[0, zt], FX + zt)
+        zr[0, zt] = pair_sum(0, zt).astype(jnp.bfloat16)
+    own(f_keep)
     each(offsets, lambda zt: got(zr.at[0, zt], FZ + zt))
     ffn = zr[0, 0].astype(jnp.float32)
     for d in range(1, line):
@@ -298,41 +311,17 @@
         xo = xg[0, z, m].astype(jnp.float32)
         out[0, m] = (xo + ffn[m * tokd:(m + 1) * tokd]).astype(jnp.bfloat16)
 
-    each(offsets, lambda zt: x_line(zt).wait_send())
-    x_line(z).wait_send()
-    x_mate().wait_send()
-    each(offsets, lambda zt: x_relay(zt).wait_send())
-    dy_mate().wait_send()
-    each(offsets, lambda zt: dy_line(zt).wait_send())
-    each(offsets, lambda zt: dy_relay(zt).wait_send())
-    dy_back().wait_send()
-    gain_back().wait_send()
-    for zt in range(line):
-        swap(0, FX, zt).wait_send()
-    for zt in inner:
-        swap(1, BX, zt).wait_send()
-    for zt in ends:
-        b_own(zt).wait_send()
-        b_other(zt).wait_send()
+    gone(xg, SX)
+    gone(dyg, SDY)
+    gone(gain, SG)
+    gone(xr, SW)
     each(offsets, lambda zt: f_out(zt).wait_send())
     got(dyn, DYB)
     got(gn, GNB)
-    for zt in range(line):
-        got(zr.at[1, zt], BZ + zt)
-    total = zr[1, 0].astype(jnp.float32)
+    got(zr.at[1], BZ)
+    gnorm = zr[1, 0].astype(jnp.float32)
     for d in range(1, line):
-        total = total + zr[1, d].astype(jnp.float32)
-    gsum[...] = total
-
-    @pl.when(z < 0)
-    def _():
-        for zt in range(line):
-            got(wr.at[zt], BW + zt)
-        total = gsum[...]
-        for d in range(line):
-            total = total + wr[d].astype(jnp.float32)
-        gsum[...] = total
-    gnorm = gsum[...]
+        gnorm = gnorm + zr[1, d].astype(jnp.float32)
     for m in range(mb):
         xo = cown[m].astype(jnp.float32)
         sc = lax.rsqrt(jnp.mean(xo * xo, axis=-1, keepdims=True) + EPS)
@@ -340,8 +329,7 @@
         mixed = jnp.mean(xo * gg, axis=-1, keepdims=True)
         gx = dyn[m].astype(jnp.float32) + sc * gg - xo * (sc * sc * sc) * mixed
         gback[0, m] = gx.astype(jnp.bfloat16)
-    for zt in inner:
-        b_out(zt).wait_send()
+    gone(zs.at[1], SB)
 
 
 def on_device(sections, tensors, carry_in, norm_gain, w_gate, w_up, w_down, tile_list, grad_in):
@@ -355,7 +343,6 @@
     bf, f32 = jnp.bfloat16, jnp.float32
     V = pltpu.VMEM
     anyspec = pl.BlockSpec(memory_space=pl.ANY)
-    nsem = 9 * line + 2
     parts = pl.pallas_call(
         functools.partial(kernel, sections, tensors),
         out_shape=[jax.ShapeDtypeStruct(carry_in.shape, bf)] * 2,
@@ -383,16 +370,14 @@
             V((2, line, per, width), bf),
             V((2, line, per, width), bf),
             V((2, line, per, width), bf),
-            V((line, per, width), bf),
-            V((per, width), f32),
             V((slots, blk, blk), bf),
             V((slots, 2 * blk, blk), bf),
             pltpu.SMEM((1, slots), jnp.int32),
             pltpu.SMEM((FB_DEV * dblocks,), jnp.int32),
             pltpu.SMEM((FB_DEV,), jnp.int32),
             pltpu.SemaphoreType.DMA((7,)),
-            pltpu.SemaphoreType.DMA((nsem,)),
-            pltpu.SemaphoreType.DMA((nsem,)),
+            pltpu.SemaphoreType.DMA((5 + line,)),
+            pltpu.SemaphoreType.DMA((5 * line + 5,)),
         ],
         compiler_params=pltpu.CompilerParams(
             collective_id=0, has_side_effects=True, vmem_limit_bytes=48 * 1024 * 1024

time: 28.4 us -> 27.8 us (0.979)
  Pallas kernels: 27.6 us -> 27 us
    pallas_call x1, Pallas kernels: 27 us -> 26.4 us  [on_device(): pl.pallas_call(functools.partial(kernel, sections, tensors), out_shape=[j...]
where the time goes in v4:
time: 27.8 us; the launch traced here: 27.7 us
  Pallas kernels  27 us (97%)
  between operations  0.64 us (2%)
    pallas_call x1, Pallas kernels, on_device(): pl.pallas_call(functools.partial(kernel, sections, tensors), out_shape=[j...  26.4 us
    pallas_call x1, Pallas kernels, on_device(): pl.pallas_call(store, out_shape=[jax.ShapeDtypeStruct(carry_in.shape, bf)...  0.65 us

profile of v4, /device:TPU:1, one launch (start us, length us, event | category | flops | bytes accessed | tf_op | source)
XLA Modules:
  0.0 27.7 jit_solution(13258278244273097195)
XLA Ops:
  0.6 26.4 %shard_map.86 = (bf16[1,2,2,4096]{3,2,1,0:T(2,128)(2,1)S(1)}, bf16[1,2,2,4096]{3,2,1,0:T(2,128)(2,1)S(1)}) custom-call(s32[1,48]{1,0:T(1,128)} %tl_h.1, bf16[1,2,2,4096]{3,2,1,0:T(2,128)(2,1)} %carry.1, f32[1,4096]{1,0:T(1,128)} %gain.1, bf16[1,48,128,128]{3,2,1,0:T(8,128)(2,1)} %wg_h.1, bf16[1,48,128,128]{3,2,1,0:T(8,128)(2,1)} %wu_h.1, ...), custom_call_target="tpu_custom_call" | custom-call | tf_op jit(solution)/shard_map/pallas_call | solution.py:346
  27.0 0.6 %shard_map.87 = (bf16[1,2,2,4096]{3,2,1,0:T(2,128)(2,1)}, bf16[1,2,2,4096]{3,2,1,0:T(2,128)(2,1)}) custom-call(bf16[1,2,2,4096]{3,2,1,0:T(2,128)(2,1)S(1)} %get-tuple-element.4.a, bf16[1,2,2,4096]{3,2,1,0:T(2,128)(2,1)S(1)} %get-tuple-element.5.b), custom_call_target="tpu_custom_call" | custom-call | tf_op jit(solution)/shard_map/pallas_call | solution.py:386

commit v5 on v4

--- a/solution.py
+++ b/solution.py
@@ -158,6 +158,15 @@
             return acc + v * v
         return lax.fori_loop(0, dblocks, body, jnp.zeros((half, blk), jnp.float32), unroll=4)
 
+    def norm(h):
+        scale = lax.rsqrt(jnp.sum(square(h), axis=-1, keepdims=True) / width + EPS)
+
+        @pl.loop(0, dblocks, unroll=4)
+        def _(c):
+            cols = pl.ds(pl.multiple_of(c * blk, blk), blk)
+            mine = slice(h * half, (h + 1) * half)
+            nb[c, mine] = (xs[c, mine] * scale * gv[:, cols]).astype(jnp.bfloat16)
+
     def pack_dy(h):
         @pl.loop(0, dblocks, unroll=4)
         def _(c):
@@ -168,10 +177,10 @@
         def _(k):
             ref[k, at:at + blk] = src[k].T
 
-    each(offsets, lambda zt: dy_line(zt).start())
     for i, (ref, src, at) in ((6, (wdt, wd, 0)), (4, (wgt, wg, 0)), (5, (wgt, wu, blk))):
         local[i].wait()
         turn(ref, src, at)
+    each(offsets, lambda zt: dy_line(zt).start())
     def relay_x(zt):
         got(xg.at[0, zt], XZ + zt)
         x_relay(zt).start()
@@ -179,22 +188,17 @@
     got(xg.at[0, z], XZ + z)
     dy_back().start()
     gain_back().start()
-    acc_own = square(0)
+    local[3].wait()
+    norm(0)
     def relay_dy(zt):
         got(dyg.at[0, zt], DYZ + zt)
         dy_relay(zt).start()
     each(offsets, relay_dy)
-    for c in local[1:4]:
+    for c in local[1:3]:
         c.wait()
     pack_dy(0)
     got(xg.at[1], XX)
-    acc = jnp.concatenate([acc_own, square(1)], axis=0)
-    scale = lax.rsqrt(jnp.sum(acc, axis=-1, keepdims=True) / width + EPS)
-
-    @pl.loop(0, dblocks, unroll=4)
-    def _(c):
-        cols = pl.ds(pl.multiple_of(c * blk, blk), blk)
-        nb[c] = (xs[c] * scale * gv[:, cols]).astype(jnp.bfloat16)
+    norm(1)
 
     def g_step(k, cur):
         w = jnp.concatenate([wg[k], wu[k]], axis=1)
@@ -209,17 +213,16 @@
         g, u = both[:, :blk], both[:, blk:]
         hb[f] = (g * jax.nn.sigmoid(g) * u).astype(jnp.bfloat16)
 
-    def collect(a):
+    def collect(a, h):
         @pl.loop(0, dblocks, unroll=4)
         def _(c):
             cols = pl.ds(pl.multiple_of(c * blk, blk), blk)
-            total = part[inv[c]]
+            mine = pl.ds(h * half, half)
+            total = part[inv[c], mine]
             for f in range(1, FB_DEV):
-                total = total + part[inv[f * dblocks + c]]
-            for h in range(PAIR):
-                for d in range(line):
-                    r = (h * line + d) * per
-                    stage[a, h, d, :, cols] = total[r:r + per].astype(jnp.bfloat16)
+                total = total + part[inv[f * dblocks + c], mine]
+            for d in range(line):
+                stage[a, h, d, :, cols] = total[d * per:(d + 1) * per].astype(jnp.bfloat16)
 
     def away(body):
         @pl.when(2 * z < line)
@@ -255,8 +258,9 @@
         part[k] = jnp.dot(hb[f_of(k)], wd[k], preferred_element_type=jnp.float32)
         return 0
     lax.fori_loop(0, slots, o_step, 0, unroll=slots)
-    collect(0)
+    collect(0, 1)
     away(lambda zt: swap(0, FX, zt).start())
+    collect(0, 0)
 
     got(dyg.at[1], DYX)
     pack_dy(1)
@@ -280,10 +284,11 @@
         part[k] = jnp.dot(dgu[f_of(k)], wgt[k], preferred_element_type=jnp.float32)
         return 0
     lax.fori_loop(0, slots, b_step, 0, unroll=slots)
-    collect(1)
+    collect(1, 1)
     away(lambda zt: swap(1, BX, zt).start())
     swap(1, BX, z).start()
     swap(0, FX, z).start()
+    collect(1, 0)
 
     def pair_sum(a, zt):
         return stage[a, 0, zt].astype(jnp.float32) + xr[a, zt].astype(jnp.float32)

time: 27.8 us -> 27.5 us (0.989)
  Pallas kernels: 27 us -> 26.7 us
    pallas_call x1, Pallas kernels: 26.4 us -> 26 us  [on_device(): pl.pallas_call(functools.partial(kernel, sections, tensors), out_shape=[j...]
where the time goes in v5:
time: 27.5 us; the launch traced here: 27.3 us
  Pallas kernels  26.7 us (97%)
  between operations  0.64 us (2%)
    pallas_call x1, Pallas kernels, on_device(): pl.pallas_call(functools.partial(kernel, sections, tensors), out_shape=[j...  26 us
    pallas_call x1, Pallas kernels, on_device(): pl.pallas_call(store, out_shape=[jax.ShapeDtypeStruct(carry_in.shape, bf)...  0.65 us

profile of v5, /device:TPU:1, one launch (start us, length us, event | category | flops | bytes accessed | tf_op | source)
XLA Modules:
  0.0 27.3 jit_solution(5876211527328910629)
XLA Ops:
  0.6 26.0 %shard_map.86 = (bf16[1,2,2,4096]{3,2,1,0:T(2,128)(2,1)S(1)}, bf16[1,2,2,4096]{3,2,1,0:T(2,128)(2,1)S(1)}) custom-call(s32[1,48]{1,0:T(1,128)} %tl_h.1, bf16[1,2,2,4096]{3,2,1,0:T(2,128)(2,1)} %carry.1, f32[1,4096]{1,0:T(1,128)} %gain.1, bf16[1,48,128,128]{3,2,1,0:T(8,128)(2,1)} %wg_h.1, bf16[1,48,128,128]{3,2,1,0:T(8,128)(2,1)} %wu_h.1, ...), custom_call_target="tpu_custom_call" | custom-call | tf_op jit(solution)/shard_map/pallas_call | solution.py:351
  26.7 0.6 %shard_map.87 = (bf16[1,2,2,4096]{3,2,1,0:T(2,128)(2,1)}, bf16[1,2,2,4096]{3,2,1,0:T(2,128)(2,1)}) custom-call(bf16[1,2,2,4096]{3,2,1,0:T(2,128)(2,1)S(1)} %get-tuple-element.4.a, bf16[1,2,2,4096]{3,2,1,0:T(2,128)(2,1)S(1)} %get-tuple-element.5.b), custom_call_target="tpu_custom_call" | custom-call | tf_op jit(solution)/shard_map/pallas_call | solution.py:391

commit v6 on v5

--- a/solution.py
+++ b/solution.py
@@ -227,7 +227,7 @@
     def away(body):
         @pl.when(2 * z < line)
         def _():
-            for zt in reversed(range(line)):
+            for zt in range(line):
                 @pl.when(z != zt)
                 def _(zt=zt):
                     body(zt)
@@ -323,16 +323,21 @@
     each(offsets, lambda zt: f_out(zt).wait_send())
     got(dyn, DYB)
     got(gn, GNB)
+    scales, cubes = [], []
+    for m in range(mb):
+        xo = cown[m].astype(jnp.float32)
+        sc = lax.rsqrt(jnp.mean(xo * xo, axis=-1, keepdims=True) + EPS)
+        scales.append(sc)
+        cubes.append(sc * sc * sc)
     got(zr.at[1], BZ)
     gnorm = zr[1, 0].astype(jnp.float32)
     for d in range(1, line):
         gnorm = gnorm + zr[1, d].astype(jnp.float32)
     for m in range(mb):
         xo = cown[m].astype(jnp.float32)
-        sc = lax.rsqrt(jnp.mean(xo * xo, axis=-1, keepdims=True) + EPS)
         gg = gn[...] * gnorm[m * tokd:(m + 1) * tokd]
         mixed = jnp.mean(xo * gg, axis=-1, keepdims=True)
-        gx = dyn[m].astype(jnp.float32) + sc * gg - xo * (sc * sc * sc) * mixed
+        gx = dyn[m].astype(jnp.float32) + scales[m] * gg - xo * (cubes[m] * mixed)
         gback[0, m] = gx.astype(jnp.bfloat16)
     gone(zs.at[1], SB)
 

time: 27.5 us -> 27.4 us (level)
  no operation moved by 1% of the time
where the time goes in v6:
time: 27.4 us; the launch traced here: 27.3 us
  Pallas kernels  26.6 us (97%)
  between operations  0.64 us (2%)
    pallas_call x1, Pallas kernels, on_device(): pl.pallas_call(functools.partial(kernel, sections, tensors), out_shape=[j...  26 us
    pallas_call x1, Pallas kernels, on_device(): pl.pallas_call(store, out_shape=[jax.ShapeDtypeStruct(carry_in.shape, bf)...  0.65 us

profile of v6, /device:TPU:1, one launch (start us, length us, event | category | flops | bytes accessed | tf_op | source)
XLA Modules:
  0.0 27.3 jit_solution(8978255613986965108)
XLA Ops:
  0.6 26.0 %shard_map.86 = (bf16[1,2,2,4096]{3,2,1,0:T(2,128)(2,1)S(1)}, bf16[1,2,2,4096]{3,2,1,0:T(2,128)(2,1)S(1)}) custom-call(s32[1,48]{1,0:T(1,128)} %tl_h.1, bf16[1,2,2,4096]{3,2,1,0:T(2,128)(2,1)} %carry.1, f32[1,4096]{1,0:T(1,128)} %gain.1, bf16[1,48,128,128]{3,2,1,0:T(8,128)(2,1)} %wg_h.1, bf16[1,48,128,128]{3,2,1,0:T(8,128)(2,1)} %wu_h.1, ...), custom_call_target="tpu_custom_call" | custom-call | tf_op jit(solution)/shard_map/pallas_call | solution.py:356
  26.6 0.6 %shard_map.87 = (bf16[1,2,2,4096]{3,2,1,0:T(2,128)(2,1)}, bf16[1,2,2,4096]{3,2,1,0:T(2,128)(2,1)}) custom-call(bf16[1,2,2,4096]{3,2,1,0:T(2,128)(2,1)S(1)} %get-tuple-element.4.a, bf16[1,2,2,4096]{3,2,1,0:T(2,128)(2,1)S(1)} %get-tuple-element.5.b), custom_call_target="tpu_custom_call" | custom-call | tf_op jit(solution)/shard_map/pallas_call | solution.py:396
